TPU v7x, 32 devices: a whole 2x2x4 slice. The times are simulated.
32 devices in a mesh: wide: 16 (over z, x, core), narrow: 2 (over y).
Axes of the slice: x: 2, y: 2, z: 4, core: 2. Of those that a mesh axis runs over, the one named last changes fastest.
Arguments:
- latents: bfloat16 [65536, 1024], P(('wide', 'narrow')), may hold values from -6 to 6
- cotangent: bfloat16 [65536, 1024], P(('wide', 'narrow')), may hold values from -6 to 6
- crop_counts: int32 [16], replicated, may hold values from 1 to 8, as said below
- image_device: int32 [16], replicated, may hold values from 0 to 15, as said below
- query_weight: bfloat16 [1024, 1024], P(None, 'narrow'), may hold values from -0.1875 to 0.1875
- key_weight: bfloat16 [1024, 1024], P(None, 'narrow'), may hold values from -0.1875 to 0.1875
- value_weight: bfloat16 [1024, 1024], P(None, 'narrow'), may hold values from -0.1875 to 0.1875
- out_weight: bfloat16 [1024, 1024], P('narrow'), may hold values from -2 to 2
- up_weight: bfloat16 [1024, 1024], P(None, 'narrow'), may hold values from -0.1875 to 0.1875
- down_weight: bfloat16 [1024, 1024], P('narrow'), may hold values from -0.1875 to 0.1875
- query_bias: bfloat16 [1024], P('narrow'), may hold values from -3 to 3
- value_bias: bfloat16 [1024], P('narrow'), may hold values from -3 to 3
- up_bias: bfloat16 [1024], P('narrow'), may hold values from -3 to 3
- out_bias: float32 [1024], replicated, may hold values from -2 to 2
- down_bias: float32 [1024], replicated, may hold values from -2 to 2
- first_gain: float32 [1024], replicated, may hold values from 0.5 to 1.5
- first_shift: float32 [1024], replicated, may hold values from -1.2 to 1.2
- second_gain: float32 [1024], replicated, may hold values from 0.5 to 1.5
- second_shift: float32 [1024], replicated, may hold values from -1.2 to 1.2
Outputs:
- block_output: bfloat16 [65536, 1024], P(('wide', 'narrow'))
- latents_gradient: float32 [65536, 1024], P(('wide', 'narrow'))
- query_weight_gradient: float32 [1024, 1024], P(None, 'narrow')
- key_weight_gradient: float32 [1024, 1024], P(None, 'narrow')
- value_weight_gradient: float32 [1024, 1024], P(None, 'narrow')
- out_weight_gradient: float32 [1024, 1024], P('narrow')
- up_weight_gradient: float32 [1024, 1024], P(None, 'narrow')
- down_weight_gradient: float32 [1024, 1024], P('narrow')
- query_bias_gradient: float32 [1024], P('narrow')
- value_bias_gradient: float32 [1024], P('narrow')
- up_bias_gradient: float32 [1024], P('narrow')
- out_bias_gradient: float32 [1024], replicated
- down_bias_gradient: float32 [1024], replicated
- first_gain_gradient: float32 [1024], replicated
- first_shift_gradient: float32 [1024], replicated
- second_gain_gradient: float32 [1024], replicated
- second_shift_gradient: float32 [1024], replicated
Inputs may be any that keep to these rules, and one draw needn't show every extreme that they name: `crop_counts`: each image holds 1 to 8 crops; the images of one wide index hold 8 crops or fewer together, and some wide index holds exactly 8. `image_device`: every wide index receives exactly one image.
All inputs are finite; a program needn't handle non-finite values.
Results may differ from a plain program's by a relative error of at most 0.02.
Values may be sent and summed in bfloat16 or wider, within the bound.
No kernel may reach another device: no remote copies, remote signals or barrier semaphores. Data moves between devices by JAX's collectives and lax.ppermute only.
A program may use at most 192 MiB of HBM per device.

v0:
```python
from functools import partial
import math
import jax
import jax.numpy as jnp
from jax import lax
from jax.sharding import PartitionSpec as P

HS = 128
CROP = 512
EPSILON = 1e-05


def normalize(values, gain, shift):
    center = values - jnp.mean(values, axis=-1, keepdims=True)
    inverse = lax.rsqrt(jnp.mean(center * center, axis=-1, keepdims=True) + EPSILON)
    unit = center * inverse
    return (unit * gain + shift, unit, inverse)


def normalize_back(upstream, unit, inverse, gain):
    scaled = upstream * gain
    inner = scaled - jnp.mean(scaled, axis=-1, keepdims=True)
    inner = inner - unit * jnp.mean(scaled * unit, axis=-1, keepdims=True)
    return (inner * inverse, jnp.sum(upstream * unit, axis=0), jnp.sum(upstream, axis=0))


def matmul(left, right):
    return jnp.dot(left, right, preferred_element_type=jnp.float32)


def matmul_left(left, right):
    return lax.dot_general(
        left, right, (((0,), (0,)), ((), ())), preferred_element_type=jnp.float32
    )


def matmul_right(left, right):
    return lax.dot_general(
        left, right, (((1,), (1,)), ((), ())), preferred_element_type=jnp.float32
    )


def crop_shape(array):
    count, width = array.shape
    return array.reshape(count // CROP, CROP, width // HS, HS)


def attend_forward(query, keys, values):
    scale = 1.0 / math.sqrt(HS)

    def one_crop(item):
        crop_query, crop_keys, crop_values = item
        scores = (
            jnp.einsum("qhd,khd->hqk", crop_query, crop_keys, preferred_element_type=jnp.float32)
            * scale
        )
        highest = jnp.max(scores, axis=-1, keepdims=True)
        weights = jnp.exp(scores - highest)
        total = jnp.sum(weights, axis=-1, keepdims=True)
        probs = (weights / total).astype(jnp.bfloat16)
        mixed = jnp.einsum("hqk,khd->qhd", probs, crop_values, preferred_element_type=jnp.float32)
        return (mixed.astype(jnp.bfloat16), (highest + jnp.log(total))[..., 0])

    mixed, logsum = lax.map(one_crop, (crop_shape(query), crop_shape(keys), crop_shape(values)))
    return (mixed.reshape(query.shape), logsum)


def attend_back(query, keys, values, logsum, upstream):
    scale = 1.0 / math.sqrt(HS)

    def one_crop(item):
        crop_query, crop_keys, crop_values, crop_logsum, crop_up = item
        scores = (
            jnp.einsum("qhd,khd->hqk", crop_query, crop_keys, preferred_element_type=jnp.float32)
            * scale
        )
        probs = jnp.exp(scores - crop_logsum[..., None])
        values_raw = jnp.einsum(
            "hqk,qhd->khd", probs.astype(jnp.bfloat16), crop_up, preferred_element_type=jnp.float32
        )
        probs_grad = jnp.einsum(
            "qhd,khd->hqk", crop_up, crop_values, preferred_element_type=jnp.float32
        )
        inner = jnp.sum(probs * probs_grad, axis=-1, keepdims=True)
        scores_grad = (probs * (probs_grad - inner)).astype(jnp.bfloat16)
        query_grad = (
            jnp.einsum("hqk,khd->qhd", scores_grad, crop_keys, preferred_element_type=jnp.float32)
            * scale
        )
        keys_grad = (
            jnp.einsum("hqk,qhd->khd", scores_grad, crop_query, preferred_element_type=jnp.float32)
            * scale
        )
        return (
            query_grad.astype(jnp.bfloat16),
            keys_grad.astype(jnp.bfloat16),
            values_raw.astype(jnp.bfloat16),
        )

    items = (crop_shape(query), crop_shape(keys), crop_shape(values), logsum, crop_shape(upstream))
    query_grad, keys_grad, values_grad = lax.map(one_crop, items)
    return (
        query_grad.reshape(query.shape),
        keys_grad.reshape(query.shape),
        values_grad.reshape(query.shape),
    )


def on_device(
    latents,
    cotangent,
    crop_counts,
    image_device,
    query_weight,
    key_weight,
    value_weight,
    out_weight,
    up_weight,
    down_weight,
    query_bias,
    value_bias,
    up_bias,
    out_bias,
    down_bias,
    first_gain,
    first_shift,
    second_gain,
    second_shift,
):
    count = latents.shape[0]
    owned = jnp.sum(jnp.where(image_device == lax.axis_index("wide"), crop_counts, 0))
    first_row = lax.axis_index("narrow") * count
    crop_index = (first_row + jnp.arange(count, dtype=jnp.int32)) // CROP
    live = (crop_index < owned).astype(jnp.float32)[:, None]
    query_full, key_full, value_full, up_full = (query_weight, key_weight, value_weight, up_weight)
    out_full, down_full = (out_weight, down_weight)
    qbias_full, vbias_full, upbias_full = (query_bias, value_bias, up_bias)
    latent_rows = latents.astype(jnp.float32)
    first_normed, first_unit, first_inverse = normalize(latent_rows, first_gain, first_shift)
    first_all = lax.all_gather(first_normed.astype(jnp.bfloat16), "narrow", axis=0, tiled=True)
    query = (matmul(first_all, query_full) + qbias_full).astype(jnp.bfloat16)
    keys = matmul(first_all, key_full).astype(jnp.bfloat16)
    values = (matmul(first_all, value_full) + vbias_full).astype(jnp.bfloat16)
    attended, logsum = attend_forward(query, keys, values)
    hidden = (
        latent_rows
        + lax.psum_scatter(
            matmul(attended, out_full).astype(jnp.bfloat16),
            "narrow",
            scatter_dimension=0,
            tiled=True,
        ).astype(jnp.float32)
        + out_bias
    )
    second_normed, second_unit, second_inverse = normalize(hidden, second_gain, second_shift)
    second_all = lax.all_gather(second_normed.astype(jnp.bfloat16), "narrow", axis=0, tiled=True)
    before = matmul(second_all, up_full) + upbias_full
    gelu_value, gelu_pull = jax.vjp(partial(jax.nn.gelu, approximate=False), before)
    activated = gelu_value.astype(jnp.bfloat16)
    result = (
        hidden
        + lax.psum_scatter(
            matmul(
                lax.dynamic_slice_in_dim(
                    activated, jnp.int32(0), lax.axis_size("narrow") * count, 0
                ),
                down_full,
            ).astype(jnp.bfloat16),
            "narrow",
            scatter_dimension=0,
            tiled=True,
        ).astype(jnp.float32)
        + down_bias
    )
    block_output = (result * live).astype(jnp.bfloat16)
    top_grad = cotangent.astype(jnp.float32) * live
    down_bias_grad = jnp.sum(top_grad, axis=0)
    top_all = lax.all_gather(top_grad.astype(jnp.bfloat16), "narrow", axis=0, tiled=True)
    down_grad = matmul_left(activated, top_all)
    activated_grad = matmul_right(top_all, down_full)
    before_grad = gelu_pull(activated_grad)[0].astype(jnp.bfloat16)
    upbias_grad = jnp.sum(before_grad.astype(jnp.float32), axis=0)
    up_grad = matmul_left(second_all, before_grad)
    second_grad = lax.psum_scatter(
        matmul_right(before_grad, up_full).astype(jnp.bfloat16),
        "narrow",
        scatter_dimension=0,
        tiled=True,
    ).astype(jnp.float32)
    hidden_part, second_gain_grad, second_shift_grad = normalize_back(
        second_grad, second_unit, second_inverse, second_gain
    )
    hidden_grad = top_grad + hidden_part
    out_bias_grad = jnp.sum(hidden_grad, axis=0)
    hidden_all = lax.all_gather(hidden_grad.astype(jnp.bfloat16), "narrow", axis=0, tiled=True)
    out_grad = matmul_left(attended, hidden_all)
    attended_grad = matmul_right(hidden_all, out_full).astype(jnp.bfloat16)
    query_grad, keys_grad, values_grad = attend_back(query, keys, values, logsum, attended_grad)
    qbias_grad = jnp.sum(query_grad.astype(jnp.float32), axis=0)
    vbias_grad = jnp.sum(values_grad.astype(jnp.float32), axis=0)
    query_wgrad = matmul_left(first_all, query_grad)
    key_wgrad = matmul_left(first_all, keys_grad)
    value_wgrad = matmul_left(first_all, values_grad)
    part = matmul_right(query_grad, query_full)
    part = part + matmul_right(keys_grad, key_full)
    first_grad = lax.psum_scatter(
        (part + matmul_right(values_grad, value_full)).astype(jnp.bfloat16),
        "narrow",
        scatter_dimension=0,
        tiled=True,
    ).astype(jnp.float32)
    input_part, first_gain_grad, first_shift_grad = normalize_back(
        first_grad, first_unit, first_inverse, first_gain
    )
    latents_gradient = hidden_grad + input_part
    matrices = (
        lax.psum(query_wgrad.astype(jnp.bfloat16), "wide").astype(jnp.float32),
        lax.psum(key_wgrad.astype(jnp.bfloat16), "wide").astype(jnp.float32),
        lax.psum(value_wgrad.astype(jnp.bfloat16), "wide").astype(jnp.float32),
        lax.psum(out_grad.astype(jnp.bfloat16), "wide").astype(jnp.float32),
        lax.psum(up_grad.astype(jnp.bfloat16), "wide").astype(jnp.float32),
        lax.psum(down_grad.astype(jnp.bfloat16), "wide").astype(jnp.float32),
        lax.psum(qbias_grad.astype(jnp.bfloat16), "wide").astype(jnp.float32),
        lax.psum(vbias_grad.astype(jnp.bfloat16), "wide").astype(jnp.float32),
        lax.psum(upbias_grad.astype(jnp.bfloat16), "wide").astype(jnp.float32),
    )
    rowwise = lax.psum(
        (
            first_gain_grad,
            first_shift_grad,
            second_gain_grad,
            second_shift_grad,
            out_bias_grad,
            down_bias_grad,
        ),
        ("wide", "narrow"),
    )
    return (
        block_output,
        latents_gradient,
        matrices[0],
        matrices[1],
        matrices[2],
        matrices[3],
        matrices[4],
        matrices[5],
        matrices[6],
        matrices[7],
        matrices[8],
        rowwise[4],
        rowwise[5],
        rowwise[0],
        rowwise[1],
        rowwise[2],
        rowwise[3],
    )


def solution(mesh):
    return jax.shard_map(
        on_device,
        mesh=mesh,
        in_specs=(
            P(("wide", "narrow"), None),
            P(("wide", "narrow"), None),
            P(),
            P(),
            P(None, "narrow"),
            P(None, "narrow"),
            P(None, "narrow"),
            P("narrow", None),
            P(None, "narrow"),
            P("narrow", None),
            P("narrow"),
            P("narrow"),
            P("narrow"),
            P(),
            P(),
            P(),
            P(),
            P(),
            P(),
        ),
        out_specs=(
            P(("wide", "narrow"), None),
            P(("wide", "narrow"), None),
            P(None, "narrow"),
            P(None, "narrow"),
            P(None, "narrow"),
            P("narrow", None),
            P(None, "narrow"),
            P("narrow", None),
            P("narrow"),
            P("narrow"),
            P("narrow"),
            P(),
            P(),
            P(),
            P(),
            P(),
            P(),
        ),
        check_vma=False,
    )
```

profile of v0, /device:TPU:0, one launch (start us, length us, event | category | flops | bytes accessed | tf_op | source)
XLA Modules:
  0.0 1423.9 jit_solution(12782932127262748092)
XLA Ops:
  17.3 106.6 %all-gather.5.cloned.1.call-done = bf16[4096,1024]{1,0:T(8,128)(2,1)} async-done(((bf16[2048,1024]{1,0:T(8,128)(2,1)}), bf16[4096,1024]{1,0:T(8,128)(2,1)}) %all-gather.5.cloned.1.call-update) | async-done | bytes 8388624 | tf_op jit(solution)/shard_map/all_gather | solution.py:140
  123.9 9.4 add_convert_fusion.3
  133.3 7.0 reshape.160
  145.6 9.4 add_convert_fusion.4
  155.0 7.0 reshape.159
  162.0 9.4 convolution_convert_fusion.4
  185.9 53.5 %while.26 = (s32[]{:T(128)}, bf16[8,512,4,128]{1,3,2,0:T(8,128)(2,1)}, f32[8,4,512]{2,1,0:T(4,128)}, bf16[8,512,4,128]{3,2,1,0:T(4,128)(2,1)}, bf16[8,512,4,128]...) while((s32[]{:T(128)}, bf16[8,512,4,128]{1,3,2,0:T(8,128)(2,1)}, f32[8,4,512]{2,1,0:T(4,128)}, ...), condition=%wide.region_5.6_spmd, body=%wide.region_2.5_spmd.sunk | while | flops 546568192 | bytes 16843872 | solution.py:64
  255.2 99.4 %reduce-scatter.5.cloned.1.call-done = bf16[2048,1024]{1,0:T(8,128)(2,1)} async-done(((bf16[4096,1024]{1,0:T(8,128)(2,1)}), bf16[2048,1024]{1,0:T(8,128)(2,1)}) %reduce-scatter.5.cloned.1.call-update) | async-done | bytes 4194320 | tf_op jit(solution)/shard_map/reduce_scatter | solution.py:147
  373.3 97.3 %all-gather.7.cloned.1.call-done = bf16[4096,1024]{1,0:T(8,128)(2,1)} async-done(((bf16[2048,1024]{1,0:T(8,128)(2,1)}), bf16[4096,1024]{1,0:T(8,128)(2,1)}) %all-gather.7.cloned.1.call-update) | async-done | bytes 8388624 | tf_op jit(solution)/shard_map/all_gather | solution.py:156
  470.6 10.3 fusion.90
  480.9 95.1 %all-gather.9.cloned.1.call-done = bf16[4096,1024]{1,0:T(8,128)(2,1)} async-done(((bf16[2048,1024]{1,0:T(8,128)(2,1)}), bf16[4096,1024]{1,0:T(8,128)(2,1)}) %all-gather.9.cloned.1.call-update) | async-done | bytes 8388624 | tf_op jit(solution)/shard_map/all_gather | solution.py:178
  576.0 27.7 %fusion.88 = (bf16[512]{0:T(512)(128)(2,1)}, bf16[4096,512]{1,0:T(8,128)(2,1)S(1)}, f32[4096,512]{1,0:T(8,128)}) fusion(f32[4096,512]{1,0:T(8,128)} %fusion.90, f32[512]{0:T(512)S(1)} %convert_element_type.173, bf16[4096,1024]{1,0:T(8,128)(2,1)} %all-gather.9.cloned.1.call-done, bf16[512,1024]{1,0:T(8,128)(2,1)S(1)} %copy-done), kind=kOutput, calls=%fused_computation.149 | convolution fusion | flops 4450156032 | bytes 30411776 | tf_op jit(solution)/shard_map/dot_general | solution.py:38
  605.6 7.2 convolution_convert_fusion
  613.1 8.0 multiply_convert_fusion.2
  630.0 82.4 %reduce-scatter.9.cloned.1.call-done = bf16[2048,1024]{1,0:T(8,128)(2,1)} async-done(((bf16[4096,1024]{1,0:T(8,128)(2,1)}), bf16[2048,1024]{1,0:T(8,128)(2,1)}) %reduce-scatter.9.cloned.1.call-update) | async-done | bytes 4194320 | tf_op jit(solution)/shard_map/reduce_scatter | solution.py:184
  712.3 8.0 fusion.70
  720.4 94.1 %reduce-scatter.7.cloned.1.call-done = bf16[2048,1024]{1,0:T(8,128)(2,1)} async-done(((bf16[4096,1024]{1,0:T(8,128)(2,1)}), bf16[2048,1024]{1,0:T(8,128)(2,1)}) %reduce-scatter.7.cloned.1.call-update) | async-done | bytes 4194320 | tf_op jit(solution)/shard_map/reduce_scatter | solution.py:162
  814.4 12.4 fusion.86
  833.0 10.3 convolution_convert_fusion.5
  843.2 9.1 convolution_convert_fusion.6
  852.3 84.7 %all-gather.11.cloned.1.call-done = bf16[4096,1024]{1,0:T(8,128)(2,1)} async-done(((bf16[2048,1024]{1,0:T(8,128)(2,1)}), bf16[4096,1024]{1,0:T(8,128)(2,1)}) %all-gather.11.cloned.1.call-update) | async-done | bytes 8388624 | tf_op jit(solution)/shard_map/all_gather | solution.py:195
  937.0 9.5 convolution_convert_fusion.3
  960.8 107.1 %while.27 = (s32[]{:T(128)}, bf16[8,512,4,128]{1,3,2,0:T(8,128)(2,1)}, bf16[8,512,4,128]{1,3,2,0:T(8,128)(2,1)}, bf16[8,512,4,128]{1,3,2,0:T(8,128)(2,1)}, bf16[...) while((s32[]{:T(128)}, ...), condition=%wide.region_16.17_spmd, body=%wide.region_14.16_spmd.sunk | while | flops 1356068864 | bytes 38857848 | solution.py:101
  1084.4 9.6 fusion.92
  1094.0 8.4 convolution_convert_fusion.7
  1119.3 10.8 fusion.91
  1130.1 18.8 %add_convert_fusion = bf16[4096,1024]{1,0:T(8,128)(2,1)} fusion(f32[4096,1024]{1,0:T(8,128)} %fusion.91, f32[4096,1024]{1,0:T(8,128)} %fusion.92, bf16[4096,512]{0,1:T(8,128)(2,1)} %bitcast.159, bf16[1024,512]{1,0:T(8,128)(2,1)S(1)} %copy-done.14), kind=kOutput, calls=%fused_computation.55 | convolution fusion | flops 4307550208 | bytes 47185920 | tf_op jit(solution)/shard_map/dot_general | solution.py:38
  1154.7 34.1 %all-reduce.1 = (bf16[512]{0:T(512)(128)(2,1)S(1)}, bf16[512]{0:T(512)(128)(2,1)S(1)}, bf16[512]{0:T(512)(128)(2,1)S(1)}) all-reduce(bf16[512]{0:T(512)(128)(2,1)S(1)} %bitcast.171, bf16[512]{0:T(512)(128)(2,1)S(1)} %bitcast.170, bf16[512]{0:T(512)(128)(2,1)S(1)} %copy-done.36), channel_id=1, replica_groups=mesh['wide'=16,'narrow'=2] {'wide'}, use_global_device_ids=true, to_apply=%region_27.28 | all-reduce | flops 1536 | bytes 6144 | tf_op jit(solution)/shard_map/psum | solution.py:223
  1190.5 68.9 %all-reduce.5.cloned.1.call-done = (bf16[1024,512]{1,0:T(8,128)(2,1)}, bf16[1024,512]{1,0:T(8,128)(2,1)}, bf16[1024,512]{1,0:T(8,128)(2,1)}, bf16[512,1024]{1,0:...) async-done(((bf16[1024,512]{1,0:T(8,128)(2,1)}, bf16[1024,512]{1,0:T(8,128)(2,1)}, bf16[1024,512]{1,0:T(8,128)(2,1)}, bf16[512,1024]{1,0:T(8,128)(2,1)}, ...) | async-done | bytes 6291472 | tf_op jit(solution)/shard_map/psum | solution.py:217
  1272.9 88.3 %reduce-scatter.11.cloned.1.call-done = bf16[2048,1024]{1,0:T(8,128)(2,1)} async-done(((bf16[4096,1024]{1,0:T(8,128)(2,1)}), bf16[2048,1024]{1,0:T(8,128)(2,1)}) %reduce-scatter.11.cloned.1.call-update) | async-done | bytes 4194320 | tf_op jit(solution)/shard_map/reduce_scatter | solution.py:206
  1367.4 40.0 %all-reduce = (f32[1024]{0:T(1024)}, f32[1024]{0:T(1024)}, f32[1024]{0:T(1024)}, f32[1024]{0:T(1024)}, f32[1024]{0:T(1024)}, /*index=5*/f32[1024]{0:T(1024)}) all-reduce(f32[1024]{0:T(1024)S(1)} %copy-done.28, f32[1024]{0:T(1024)S(1)} %copy-done.29, ...), channel_id=1, replica_groups=mesh['wide'=16,'narrow'=2] {'wide','narrow'}, use_global_device_ids=true, to_apply=%region_33.34 | all-reduce | flops 6144 | bytes 49152 | tf_op jit(solution)/shard_map/psum | solution.py:227
  1407.3 9.5 fusion.61
  (285 shorter events, 315.5 us)
Async XLA Ops:
  7.2 568.8 %copy-start = (bf16[512,1024]{1,0:T(8,128)(2,1)S(1)}, bf16[512,1024]{1,0:T(8,128)(2,1)}, u32[]{:S(2)}) copy-start(bf16[512,1024]{1,0:T(8,128)(2,1)} %param.32) | copy-start | bytes 3145732
  7.2 116.7 %all-gather.5.cloned.1.call-start = ((), (), s32[]{:S(2)}) async-start(), calls=%async_computation.4 | async-start | bytes 12582912 | tf_op jit(solution)/shard_map/all_gather | solution.py:140
  10.3 113.6 %copy-start.44 = (bf16[1024,512]{1,0:T(8,128)(2,1)S(1)}, bf16[1024,512]{1,0:T(8,128)(2,1)}, u32[]{:S(2)}) copy-start(bf16[1024,512]{1,0:T(8,128)(2,1)} %param.27) | copy-start | bytes 3145732
  17.0 337.6 %reduce-scatter.5.cloned.1.call-start = ((), (), s32[]{:S(2)}) async-start(), calls=%async_computation.5 | async-start | bytes 12582912 | tf_op jit(solution)/shard_map/reduce_scatter | solution.py:147
  133.3 12.3 copy-start.13
  255.1 99.5 %copy-start.22 = (f32[1024]{0:T(1024)S(1)}, f32[1024]{0:T(1024)}, u32[]{:S(2)}) copy-start(f32[1024]{0:T(1024)} %param.36) | copy-start | bytes 12292
  255.2 107.5 %copy-start.25 = (f32[1024]{0:T(1024)S(1)}, f32[1024]{0:T(1024)}, u32[]{:S(2)}) copy-start(f32[1024]{0:T(1024)} %param.40) | copy-start | bytes 12292
  255.2 107.5 %copy-start.31 = (f32[1024]{0:T(1024)S(1)}, f32[1024]{0:T(1024)}, u32[]{:S(2)}) copy-start(f32[1024]{0:T(1024)} %param.41) | copy-start | bytes 12292
  255.2 215.4 %all-gather.7.cloned.1.call-start = ((), (), s32[]{:S(2)}) async-start(), calls=%async_computation.6 | async-start | bytes 12582912 | tf_op jit(solution)/shard_map/all_gather | solution.py:156
  366.4 104.2 %copy-start.39 = (bf16[1024,512]{1,0:T(8,128)(2,1)S(1)}, bf16[1024,512]{1,0:T(8,128)(2,1)}, u32[]{:S(2)}) copy-start(bf16[1024,512]{1,0:T(8,128)(2,1)} %param.31) | copy-start | bytes 3145732
  366.5 209.5 %all-gather.9.cloned.1.call-start = ((), (), s32[]{:S(2)}) async-start(), calls=%async_computation.8 | async-start | bytes 12582912 | tf_op jit(solution)/shard_map/all_gather | solution.py:178
  372.7 339.6 %reduce-scatter.9.cloned.1.call-start = ((), (), s32[]{:S(2)}) async-start(), calls=%async_computation.9 | async-start | bytes 12582912 | tf_op jit(solution)/shard_map/reduce_scatter | solution.py:184
  612.8 201.6 %reduce-scatter.7.cloned.1.call-start = ((), (), s32[]{:S(2)}) async-start(), calls=%async_computation.7 | async-start | bytes 12582912 | tf_op jit(solution)/shard_map/reduce_scatter | solution.py:162
  629.9 184.5 %copy-start.32 = (f32[1024]{0:T(1024)S(1)}, f32[1024]{0:T(1024)}, u32[]{:S(2)}) copy-start(f32[1024]{0:T(1024)} %param.37) | copy-start | bytes 12292
  629.9 307.1 %all-gather.11.cloned.1.call-start = ((), (), s32[]{:S(2)}) async-start(), calls=%async_computation.10 | async-start | bytes 12582912 | tf_op jit(solution)/shard_map/all_gather | solution.py:195
  832.9 426.5 %all-reduce.5.cloned.1.call-start = ((), (), s32[]{:S(2)}) async-start(), calls=%async_computation.12 | async-start | bytes 12582912 | tf_op jit(solution)/shard_map/psum | solution.py:217
  843.2 93.8 %copy-start.41 = (bf16[512,1024]{1,0:T(8,128)(2,1)S(1)}, bf16[512,1024]{1,0:T(8,128)(2,1)}, u32[]{:S(2)}) copy-start(bf16[512,1024]{1,0:T(8,128)(2,1)} %param.30) | copy-start | bytes 3145732
  1079.5 33.9 %copy-start.8 = (bf16[64,8,8,512]{3,1,2,0:T(8,128)(2,1)}, bf16[64,8,8,512]{3,1,2,0:T(8,128)(2,1)S(1)}, u32[]{:S(2)}) copy-start(bf16[64,8,8,512]{3,1,2,0:T(8,128)(2,1)S(1)} %copy.81) | copy-start | bytes 12582916
  1084.4 23.5 %copy-start.11 = (bf16[64,8,8,512]{3,1,2,0:T(8,128)(2,1)}, bf16[64,8,8,512]{3,1,2,0:T(8,128)(2,1)S(1)}, u32[]{:S(2)}) copy-start(bf16[64,8,8,512]{3,1,2,0:T(8,128)(2,1)S(1)} %copy.79) | copy-start | bytes 12582916
  1084.4 17.9 %slice-start = ((s8[8388608]{0:T(1024)(128)(4,1)}), s8[4194304]{0:T(1024)(128)(4,1)S(1)}, s32[]{:S(2)}) async-start(s8[8388608]{0:T(1024)(128)(4,1)} %bitcast.172), calls=%async_computation.13 | async-start | bytes 8388608
  1119.3 10.9 copy-start.14
  1119.3 241.9 %reduce-scatter.11.cloned.1.call-start = ((), (), s32[]{:S(2)}) async-start(), calls=%async_computation.11 | async-start | bytes 12582912 | tf_op jit(solution)/shard_map/reduce_scatter | solution.py:206
  1259.4 10.3 copy-start.16
  1259.4 11.9 copy-start.15
  1262.4 98.8 %copy-start.19 = (f32[2048]{0:T(1024)S(1)}, f32[2048]{0:T(1024)}, u32[]{:S(2)}) copy-start(f32[2048]{0:T(1024)} %copy-done.18) | copy-start | bytes 24580
  1262.4 98.8 %copy-start.21 = (f32[2048]{0:T(1024)S(1)}, f32[2048]{0:T(1024)}, u32[]{:S(2)}) copy-start(f32[2048]{0:T(1024)} %copy-done.20) | copy-start | bytes 24580
  1262.4 98.8 %copy-start.24 = (f32[1024]{0:T(1024)S(1)}, f32[1024]{0:T(1024)}, u32[]{:S(2)}) copy-start(f32[1024]{0:T(1024)} %param.38) | copy-start | bytes 12292
  1268.1 99.2 %copy-start.26 = (f32[1024]{0:T(1024)S(1)}, f32[1024]{0:T(1024)}, u32[]{:S(2)}) copy-start(f32[1024]{0:T(1024)} %get-tuple-element.134) | copy-start | bytes 12292
  1268.1 99.2 %copy-start.27 = (f32[1024]{0:T(1024)S(1)}, f32[1024]{0:T(1024)}, u32[]{:S(2)}) copy-start(f32[1024]{0:T(1024)} %get-tuple-element.140) | copy-start | bytes 12292
  1268.1 99.2 %copy-start.28 = (f32[1024]{0:T(1024)S(1)}, f32[1024]{0:T(1024)}, u32[]{:S(2)}) copy-start(f32[1024]{0:T(1024)} %get-tuple-element.187) | copy-start | bytes 12292
  1268.1 99.2 %copy-start.29 = (f32[1024]{0:T(1024)S(1)}, f32[1024]{0:T(1024)}, u32[]{:S(2)}) copy-start(f32[1024]{0:T(1024)} %get-tuple-element.199) | copy-start | bytes 12292
  1367.3 49.5 %copy-start.1 = (bf16[512,1024]{1,0:T(8,128)(2,1)S(1)}, bf16[512,1024]{1,0:T(8,128)(2,1)}, u32[]{:S(2)}) copy-start(bf16[512,1024]{1,0:T(8,128)(2,1)} %param.32) | copy-start | bytes 3145732
  (27 other events, 153.8 us)
Sparse Core Ops, SparseCore 0:
  17.1 106.6 all-gather.4
  255.3 99.3 reduce-scatter.4
  366.6 103.9 all-gather.6
  472.0 103.9 all-gather.8
  613.0 99.3 reduce-scatter.8
  715.1 99.3 reduce-scatter.6
  833.0 103.9 all-gather.10
  1119.4 139.9 all-reduce.4
  1261.7 99.4 reduce-scatter.10
where the time goes:
time: 1430 us; the launch traced here: 1420 us
  waiting for transfers between devices  817 us (57%)
  matrix products  289 us (20%)
  other arithmetic  114 us (8%)
  local copies, waits for them, and re-layouts  113 us (8%)
  blocking collectives  74.1 us (5%)
  between operations  15 us (1%)
    all_gather x1, waiting for transfers between devices, on_device(): lax.all_gather(first_normed.astype(jnp.bfloat16), 'narrow', axis=0, tiled...  107 us
    reduce_scatter x1, waiting for transfers between devices, on_device(): lax.psum_scatter(matmul(attended, out_full).astype(jnp.bfloat16), 'narrow...  99.4 us
    all_gather x1, waiting for transfers between devices, on_device(): lax.all_gather(second_normed.astype(jnp.bfloat16), 'narrow', axis=0, tile...  97.3 us
    all_gather x1, waiting for transfers between devices, on_device(): lax.all_gather(top_grad.astype(jnp.bfloat16), 'narrow', axis=0, tiled=True)  95.1 us
    reduce_scatter x1, waiting for transfers between devices, on_device(): lax.psum_scatter(matmul(lax.dynamic_slice_in_dim(activated, jnp.int32(0),...  94.1 us
    reduce_scatter x1, waiting for transfers between devices, on_device(): lax.psum_scatter((part + matmul_right(values_grad, value_full)).astype(jn...  88.3 us
    all_gather x1, waiting for transfers between devices, on_device(): lax.all_gather(hidden_grad.astype(jnp.bfloat16), 'narrow', axis=0, tiled=...  84.7 us
    dot_general x6, matrix products, matmul_right(): lax.dot_general(left, right, (((1,), (1,)), ((), ())), preferred_element_...  83.6 us
  transfers between devices with their start and end apart: 9, of which 9 were waited for; matrix products, arithmetic and copies ran while one was open for 8% of the time, Pallas kernels for 0%

commit v1 on v0

--- a/solution.py
+++ b/solution.py
@@ -8,6 +8,12 @@
 HS = 128
 CROP = 512
 EPSILON = 1e-05
+
+
+def add_all(block, name):
+    pieces = lax.all_gather(block, name, axis=0, tiled=False)
+    acc = pieces.sum(axis=0)
+    return acc
 
 
 def normalize(values, gain, shift):
@@ -220,7 +226,7 @@
         lax.psum(out_grad.astype(jnp.bfloat16), "wide").astype(jnp.float32),
         lax.psum(up_grad.astype(jnp.bfloat16), "wide").astype(jnp.float32),
         lax.psum(down_grad.astype(jnp.bfloat16), "wide").astype(jnp.float32),
-        lax.psum(qbias_grad.astype(jnp.bfloat16), "wide").astype(jnp.float32),
+        add_all(qbias_grad.astype(jnp.bfloat16), "wide").astype(jnp.float32),
         lax.psum(vbias_grad.astype(jnp.bfloat16), "wide").astype(jnp.float32),
         lax.psum(upbias_grad.astype(jnp.bfloat16), "wide").astype(jnp.float32),
     )

time: 1430 us -> 1430 us (level)
  blocking collectives: 74.1 us -> 91.3 us
  waiting for transfers between devices: 817 us -> 800 us
    all_gather x0 -> x1, blocking collectives: none -> 17.4 us  [add_all(): pieces = lax.all_gather(block, name, axis=0, tiled=False)]
    psum x1, waiting for transfers between devices: 68.9 us -> 51.5 us  [on_device(): lax.psum(query_wgrad.astype(jnp.bfloat16), 'wide').astype(jnp.float32)]
where the time goes in v1:
time: 1430 us; the launch traced here: 1420 us
  waiting for transfers between devices  800 us (56%)
  matrix products  289 us (20%)
  other arithmetic  114 us (8%)
  local copies, waits for them, and re-layouts  113 us (8%)
  blocking collectives  91.3 us (6%)
  between operations  15 us (1%)
    all_gather x1, waiting for transfers between devices, on_device(): lax.all_gather(first_normed.astype(jnp.bfloat16), 'narrow', axis=0, tiled...  107 us
    reduce_scatter x1, waiting for transfers between devices, on_device(): lax.psum_scatter(matmul(attended, out_full).astype(jnp.bfloat16), 'narrow...  99.4 us
    all_gather x1, waiting for transfers between devices, on_device(): lax.all_gather(second_normed.astype(jnp.bfloat16), 'narrow', axis=0, tile...  97.3 us
    all_gather x1, waiting for transfers between devices, on_device(): lax.all_gather(top_grad.astype(jnp.bfloat16), 'narrow', axis=0, tiled=True)  95.2 us
    reduce_scatter x1, waiting for transfers between devices, on_device(): lax.psum_scatter(matmul(lax.dynamic_slice_in_dim(activated, jnp.int32(0),...  94.1 us
    reduce_scatter x1, waiting for transfers between devices, on_device(): lax.psum_scatter((part + matmul_right(values_grad, value_full)).astype(jn...  88.3 us
    all_gather x1, waiting for transfers between devices, on_device(): lax.all_gather(hidden_grad.astype(jnp.bfloat16), 'narrow', axis=0, tiled=...  84.7 us
    dot_general x6, matrix products, matmul_right(): lax.dot_general(left, right, (((1,), (1,)), ((), ())), preferred_element_...  83.5 us
  transfers between devices with their start and end apart: 9, of which 9 were waited for; matrix products, arithmetic and copies ran while one was open for 8% of the time, Pallas kernels for 0%

profile of v1, /device:TPU:0, one launch (start us, length us, event | category | flops | bytes accessed | tf_op | source)
XLA Modules:
  0.0 1424.1 jit_solution(4943126281354545208)
XLA Ops:
  17.3 106.6 %all-gather.6.cloned.1.call-done = bf16[4096,1024]{1,0:T(8,128)(2,1)} async-done(((bf16[2048,1024]{1,0:T(8,128)(2,1)}), bf16[4096,1024]{1,0:T(8,128)(2,1)}) %all-gather.6.cloned.1.call-update) | async-done | bytes 8388624 | tf_op jit(solution)/shard_map/all_gather | solution.py:146
  123.9 9.4 add_convert_fusion.3
  145.5 9.4 add_convert_fusion.4
  155.0 7.0 reshape.160
  161.9 9.4 convolution_convert_fusion.4
  185.9 53.5 %while.26 = (s32[]{:T(128)}, bf16[8,512,4,128]{1,3,2,0:T(8,128)(2,1)}, f32[8,4,512]{2,1,0:T(4,128)}, bf16[8,512,4,128]{3,2,1,0:T(4,128)(2,1)}, bf16[8,512,4,128]...) while((s32[]{:T(128)}, bf16[8,512,4,128]{1,3,2,0:T(8,128)(2,1)}, f32[8,4,512]{2,1,0:T(4,128)}, ...), condition=%wide.region_5.6_spmd, body=%wide.region_2.5_spmd.sunk | while | flops 546568192 | bytes 16843872 | solution.py:70
  255.2 99.4 %reduce-scatter.5.cloned.1.call-done = bf16[2048,1024]{1,0:T(8,128)(2,1)} async-done(((bf16[4096,1024]{1,0:T(8,128)(2,1)}), bf16[2048,1024]{1,0:T(8,128)(2,1)}) %reduce-scatter.5.cloned.1.call-update) | async-done | bytes 4194320 | tf_op jit(solution)/shard_map/reduce_scatter | solution.py:153
  373.2 97.3 %all-gather.8.cloned.1.call-done = bf16[4096,1024]{1,0:T(8,128)(2,1)} async-done(((bf16[2048,1024]{1,0:T(8,128)(2,1)}), bf16[4096,1024]{1,0:T(8,128)(2,1)}) %all-gather.8.cloned.1.call-update) | async-done | bytes 8388624 | tf_op jit(solution)/shard_map/all_gather | solution.py:162
  470.6 10.3 fusion.90
  480.8 95.2 %all-gather.10.cloned.1.call-done = bf16[4096,1024]{1,0:T(8,128)(2,1)} async-done(((bf16[2048,1024]{1,0:T(8,128)(2,1)}), bf16[4096,1024]{1,0:T(8,128)(2,1)}) %all-gather.10.cloned.1.call-update) | async-done | bytes 8388624 | tf_op jit(solution)/shard_map/all_gather | solution.py:184
  576.0 27.7 %fusion.88 = (bf16[512]{0:T(512)(128)(2,1)}, bf16[4096,512]{1,0:T(8,128)(2,1)S(1)}, f32[4096,512]{1,0:T(8,128)}) fusion(f32[4096,512]{1,0:T(8,128)} %fusion.90, f32[512]{0:T(512)S(1)} %convert_element_type.175, bf16[4096,1024]{1,0:T(8,128)(2,1)} %all-gather.10.cloned.1.call-done, bf16[512,1024]{1,0:T(8,128)(2,1)S(1)} %copy-done), kind=kOutput, calls=%fused_computation.149 | convolution fusion | flops 4450156032 | bytes 30411776 | tf_op jit(solution)/shard_map/dot_general | solution.py:44
  605.6 7.2 convolution_convert_fusion
  613.0 8.0 multiply_convert_fusion.2
  629.9 82.4 %reduce-scatter.9.cloned.1.call-done = bf16[2048,1024]{1,0:T(8,128)(2,1)} async-done(((bf16[4096,1024]{1,0:T(8,128)(2,1)}), bf16[2048,1024]{1,0:T(8,128)(2,1)}) %reduce-scatter.9.cloned.1.call-update) | async-done | bytes 4194320 | tf_op jit(solution)/shard_map/reduce_scatter | solution.py:190
  712.3 8.0 fusion.70
  720.3 94.1 %reduce-scatter.7.cloned.1.call-done = bf16[2048,1024]{1,0:T(8,128)(2,1)} async-done(((bf16[4096,1024]{1,0:T(8,128)(2,1)}), bf16[2048,1024]{1,0:T(8,128)(2,1)}) %reduce-scatter.7.cloned.1.call-update) | async-done | bytes 4194320 | tf_op jit(solution)/shard_map/reduce_scatter | solution.py:168
  814.4 12.4 fusion.86
  832.9 10.3 convolution_convert_fusion.5
  843.2 9.1 convolution_convert_fusion.6
  852.3 84.7 %all-gather.12.cloned.1.call-done = bf16[4096,1024]{1,0:T(8,128)(2,1)} async-done(((bf16[2048,1024]{1,0:T(8,128)(2,1)}), bf16[4096,1024]{1,0:T(8,128)(2,1)}) %all-gather.12.cloned.1.call-update) | async-done | bytes 8388624 | tf_op jit(solution)/shard_map/all_gather | solution.py:201
  937.0 9.5 convolution_convert_fusion.3
  960.8 107.2 %while.27 = (s32[]{:T(128)}, bf16[8,512,4,128]{1,3,2,0:T(8,128)(2,1)}, bf16[8,512,4,128]{1,3,2,0:T(8,128)(2,1)}, bf16[8,512,4,128]{1,3,2,0:T(8,128)(2,1)}, bf16[...) while((s32[]{:T(128)}, ...), condition=%wide.region_16.17_spmd, body=%wide.region_14.16_spmd.sunk | while | flops 1356068864 | bytes 38857848 | solution.py:107
  1084.5 9.6 fusion.92
  1094.0 8.4 convolution_convert_fusion.7
  1119.3 10.8 fusion.91
  1130.2 18.8 %add_convert_fusion = bf16[4096,1024]{1,0:T(8,128)(2,1)} fusion(f32[4096,1024]{1,0:T(8,128)} %fusion.91, f32[4096,1024]{1,0:T(8,128)} %fusion.92, bf16[4096,512]{0,1:T(8,128)(2,1)} %bitcast.158, bf16[1024,512]{1,0:T(8,128)(2,1)S(1)} %copy-done.14), kind=kOutput, calls=%fused_computation.55 | convolution fusion | flops 4307550208 | bytes 47185920 | tf_op jit(solution)/shard_map/dot_general | solution.py:44
  1154.8 33.9 %all-reduce.1 = (bf16[512]{0:T(512)(128)(2,1)S(1)}, bf16[512]{0:T(512)(128)(2,1)S(1)}) all-reduce(bf16[512]{0:T(512)(128)(2,1)S(1)} %bitcast.169, bf16[512]{0:T(512)(128)(2,1)S(1)} %copy-done.36), channel_id=1, replica_groups=mesh['wide'=16,'narrow'=2] {'wide'}, use_global_device_ids=true, to_apply=%region_29.30 | all-reduce | flops 1024 | bytes 4096 | tf_op jit(solution)/shard_map/psum | solution.py:230
  1189.8 17.4 %all-gather = bf16[16,1,512]{2,1,0:T(2,128)(2,1)S(1)} all-gather(bf16[1,1,512]{2,1,0:T(2,128)(2,1)S(1)} %reshape.168), channel_id=1, replica_groups=mesh['wide'=16,'narrow'=2] {'wide'}, dimensions={0}, use_global_device_ids=true | all-gather | bytes 17408 | tf_op jit(solution)/shard_map/all_gather | solution.py:14
  1207.9 51.5 %all-reduce.5.cloned.1.call-done = (bf16[1024,512]{1,0:T(8,128)(2,1)}, bf16[1024,512]{1,0:T(8,128)(2,1)}, bf16[1024,512]{1,0:T(8,128)(2,1)}, bf16[512,1024]{1,0:...) async-done(((bf16[1024,512]{1,0:T(8,128)(2,1)}, bf16[1024,512]{1,0:T(8,128)(2,1)}, bf16[1024,512]{1,0:T(8,128)(2,1)}, bf16[512,1024]{1,0:T(8,128)(2,1)}, ...) | async-done | bytes 6291472 | tf_op jit(solution)/shard_map/psum | solution.py:223
  1272.8 88.3 %reduce-scatter.11.cloned.1.call-done = bf16[2048,1024]{1,0:T(8,128)(2,1)} async-done(((bf16[4096,1024]{1,0:T(8,128)(2,1)}), bf16[2048,1024]{1,0:T(8,128)(2,1)}) %reduce-scatter.11.cloned.1.call-update) | async-done | bytes 4194320 | tf_op jit(solution)/shard_map/reduce_scatter | solution.py:212
  1367.6 40.0 %all-reduce = (f32[1024]{0:T(1024)}, f32[1024]{0:T(1024)}, f32[1024]{0:T(1024)}, f32[1024]{0:T(1024)}, f32[1024]{0:T(1024)}, /*index=5*/f32[1024]{0:T(1024)}) all-reduce(f32[1024]{0:T(1024)S(1)} %copy-done.28, f32[1024]{0:T(1024)S(1)} %copy-done.29, ...), channel_id=1, replica_groups=mesh['wide'=16,'narrow'=2] {'wide','narrow'}, use_global_device_ids=true, to_apply=%region_33.34 | all-reduce | flops 6144 | bytes 49152 | tf_op jit(solution)/shard_map/psum | solution.py:233
  1407.5 9.5 fusion.61
  (288 shorter events, 322.8 us)
Async XLA Ops:
  7.2 568.8 %copy-start = (bf16[512,1024]{1,0:T(8,128)(2,1)S(1)}, bf16[512,1024]{1,0:T(8,128)(2,1)}, u32[]{:S(2)}) copy-start(bf16[512,1024]{1,0:T(8,128)(2,1)} %param.32) | copy-start | bytes 3145732
  7.2 116.7 %all-gather.6.cloned.1.call-start = ((), (), s32[]{:S(2)}) async-start(), calls=%async_computation.4 | async-start | bytes 12582912 | tf_op jit(solution)/shard_map/all_gather | solution.py:146
  10.3 113.6 %copy-start.44 = (bf16[1024,512]{1,0:T(8,128)(2,1)S(1)}, bf16[1024,512]{1,0:T(8,128)(2,1)}, u32[]{:S(2)}) copy-start(bf16[1024,512]{1,0:T(8,128)(2,1)} %param.27) | copy-start | bytes 3145732
  17.0 337.6 %reduce-scatter.5.cloned.1.call-start = ((), (), s32[]{:S(2)}) async-start(), calls=%async_computation.5 | async-start | bytes 12582912 | tf_op jit(solution)/shard_map/reduce_scatter | solution.py:153
  133.3 12.2 copy-start.13
  255.1 99.5 %copy-start.22 = (f32[1024]{0:T(1024)S(1)}, f32[1024]{0:T(1024)}, u32[]{:S(2)}) copy-start(f32[1024]{0:T(1024)} %param.36) | copy-start | bytes 12292
  255.1 107.5 %copy-start.25 = (f32[1024]{0:T(1024)S(1)}, f32[1024]{0:T(1024)}, u32[]{:S(2)}) copy-start(f32[1024]{0:T(1024)} %param.40) | copy-start | bytes 12292
  255.2 107.5 %copy-start.31 = (f32[1024]{0:T(1024)S(1)}, f32[1024]{0:T(1024)}, u32[]{:S(2)}) copy-start(f32[1024]{0:T(1024)} %param.41) | copy-start | bytes 12292
  255.2 215.4 %all-gather.8.cloned.1.call-start = ((), (), s32[]{:S(2)}) async-start(), calls=%async_computation.6 | async-start | bytes 12582912 | tf_op jit(solution)/shard_map/all_gather | solution.py:162
  366.4 104.2 %copy-start.39 = (bf16[1024,512]{1,0:T(8,128)(2,1)S(1)}, bf16[1024,512]{1,0:T(8,128)(2,1)}, u32[]{:S(2)}) copy-start(bf16[1024,512]{1,0:T(8,128)(2,1)} %param.31) | copy-start | bytes 3145732
  366.4 209.6 %all-gather.10.cloned.1.call-start = ((), (), s32[]{:S(2)}) async-start(), calls=%async_computation.8 | async-start | bytes 12582912 | tf_op jit(solution)/shard_map/all_gather | solution.py:184
  372.7 339.6 %reduce-scatter.9.cloned.1.call-start = ((), (), s32[]{:S(2)}) async-start(), calls=%async_computation.9 | async-start | bytes 12582912 | tf_op jit(solution)/shard_map/reduce_scatter | solution.py:190
  612.8 201.6 %reduce-scatter.7.cloned.1.call-start = ((), (), s32[]{:S(2)}) async-start(), calls=%async_computation.7 | async-start | bytes 12582912 | tf_op jit(solution)/shard_map/reduce_scatter | solution.py:168
  629.9 184.5 %copy-start.32 = (f32[1024]{0:T(1024)S(1)}, f32[1024]{0:T(1024)}, u32[]{:S(2)}) copy-start(f32[1024]{0:T(1024)} %param.37) | copy-start | bytes 12292
  629.9 307.1 %all-gather.12.cloned.1.call-start = ((), (), s32[]{:S(2)}) async-start(), calls=%async_computation.10 | async-start | bytes 12582912 | tf_op jit(solution)/shard_map/all_gather | solution.py:201
  832.9 426.5 %all-reduce.5.cloned.1.call-start = ((), (), s32[]{:S(2)}) async-start(), calls=%async_computation.12 | async-start | bytes 12582912 | tf_op jit(solution)/shard_map/psum | solution.py:223
  843.2 93.8 %copy-start.41 = (bf16[512,1024]{1,0:T(8,128)(2,1)S(1)}, bf16[512,1024]{1,0:T(8,128)(2,1)}, u32[]{:S(2)}) copy-start(bf16[512,1024]{1,0:T(8,128)(2,1)} %param.30) | copy-start | bytes 3145732
  1079.6 33.9 %copy-start.8 = (bf16[64,8,8,512]{3,1,2,0:T(8,128)(2,1)}, bf16[64,8,8,512]{3,1,2,0:T(8,128)(2,1)S(1)}, u32[]{:S(2)}) copy-start(bf16[64,8,8,512]{3,1,2,0:T(8,128)(2,1)S(1)} %copy.99) | copy-start | bytes 12582916
  1084.4 23.5 %copy-start.11 = (bf16[64,8,8,512]{3,1,2,0:T(8,128)(2,1)}, bf16[64,8,8,512]{3,1,2,0:T(8,128)(2,1)S(1)}, u32[]{:S(2)}) copy-start(bf16[64,8,8,512]{3,1,2,0:T(8,128)(2,1)S(1)} %copy.97) | copy-start | bytes 12582916
  1084.5 17.9 %slice-start = ((s8[8388608]{0:T(1024)(128)(4,1)}), s8[4194304]{0:T(1024)(128)(4,1)S(1)}, s32[]{:S(2)}) async-start(s8[8388608]{0:T(1024)(128)(4,1)} %bitcast.170), calls=%async_computation.13 | async-start | bytes 8388608
  1119.3 10.9 copy-start.14
  1119.3 241.9 %reduce-scatter.11.cloned.1.call-start = ((), (), s32[]{:S(2)}) async-start(), calls=%async_computation.11 | async-start | bytes 12582912 | tf_op jit(solution)/shard_map/reduce_scatter | solution.py:212
  1259.3 10.3 copy-start.16
  1259.3 11.9 copy-start.15
  1262.3 98.8 %copy-start.19 = (f32[2048]{0:T(1024)S(1)}, f32[2048]{0:T(1024)}, u32[]{:S(2)}) copy-start(f32[2048]{0:T(1024)} %copy-done.18) | copy-start | bytes 24580
  1262.3 98.8 %copy-start.21 = (f32[2048]{0:T(1024)S(1)}, f32[2048]{0:T(1024)}, u32[]{:S(2)}) copy-start(f32[2048]{0:T(1024)} %copy-done.20) | copy-start | bytes 24580
  1262.3 98.8 %copy-start.24 = (f32[1024]{0:T(1024)S(1)}, f32[1024]{0:T(1024)}, u32[]{:S(2)}) copy-start(f32[1024]{0:T(1024)} %param.38) | copy-start | bytes 12292
  1268.1 99.5 %copy-start.26 = (f32[1024]{0:T(1024)S(1)}, f32[1024]{0:T(1024)}, u32[]{:S(2)}) copy-start(f32[1024]{0:T(1024)} %get-tuple-element.149) | copy-start | bytes 12292
  1268.1 99.5 %copy-start.27 = (f32[1024]{0:T(1024)S(1)}, f32[1024]{0:T(1024)}, u32[]{:S(2)}) copy-start(f32[1024]{0:T(1024)} %get-tuple-element.155) | copy-start | bytes 12292
  1268.1 99.5 %copy-start.28 = (f32[1024]{0:T(1024)S(1)}, f32[1024]{0:T(1024)}, u32[]{:S(2)}) copy-start(f32[1024]{0:T(1024)} %get-tuple-element.201) | copy-start | bytes 12292
  1268.1 99.5 %copy-start.29 = (f32[1024]{0:T(1024)S(1)}, f32[1024]{0:T(1024)}, u32[]{:S(2)}) copy-start(f32[1024]{0:T(1024)} %get-tuple-element.213) | copy-start | bytes 12292
  1367.6 49.5 %copy-start.1 = (bf16[512,1024]{1,0:T(8,128)(2,1)S(1)}, bf16[512,1024]{1,0:T(8,128)(2,1)}, u32[]{:S(2)}) copy-start(bf16[512,1024]{1,0:T(8,128)(2,1)} %param.32) | copy-start | bytes 3145732
  (27 other events, 153.8 us)
Sparse Core Ops, SparseCore 0:
  17.1 106.6 all-gather.5
  255.3 99.3 reduce-scatter.4
  366.6 103.9 all-gather.7
  472.0 103.9 all-gather.9
  612.9 99.3 reduce-scatter.8
  715.0 99.3 reduce-scatter.6
  833.0 103.9 all-gather.11
  1119.4 139.8 all-reduce.4
  1261.6 99.4 reduce-scatter.10
